TPU v7x, 32 devices: a whole 2x2x4 slice. The times are simulated.
32 devices in a mesh: fsdp: 4 (over z), ctx: 4 (over x, core), tensor: 2 (over y).
Axes of the slice: x: 2, y: 2, z: 4, core: 2. Of those that a mesh axis runs over, the one named last changes fastest.
Arguments:
- tokens_in: bfloat16 [16384, 2048], P(('fsdp', 'ctx', 'tensor')), may hold values from -6 to 6
- attn_gain: float32 [2048], replicated, may hold values from 0.5 to 1.5
- query_weight: bfloat16 [2048, 2048], P('fsdp', 'tensor'), may hold values from -0.1875 to 0.1875
- key_weight: bfloat16 [2048, 2048], P('fsdp', 'tensor'), may hold values from -0.1875 to 0.1875
- value_weight: bfloat16 [2048, 2048], P('fsdp', 'tensor'), may hold values from -0.125 to 0.125
- output_weight: bfloat16 [2048, 2048], P('fsdp', 'tensor'), may hold values from -1 to 1
- mlp_gain: float32 [2048], replicated, may hold values from 0.5 to 1.5
- gate_weight: bfloat16 [2048, 8192], P('fsdp', 'tensor'), may hold values from -0.125 to 0.125
- up_weight: bfloat16 [2048, 8192], P('fsdp', 'tensor'), may hold values from -0.125 to 0.125
- down_weight: bfloat16 [2048, 8192], P('fsdp', 'tensor'), may hold values from -0.0625 to 0.0625
- seg_lengths: int32 [4, 20], P('fsdp'), may hold values from 1 to 128, 1920 in all within a row
- leaf_parent: int32 [4, 16], P('fsdp'), may hold values from 1 to 4
- cotangent: bfloat16 [16384, 2048], P(('fsdp', 'ctx', 'tensor')), may hold values from -6 to 6
Outputs:
- block_out: bfloat16 [16384, 2048], P(('fsdp', 'ctx', 'tensor'))
- input_grad: bfloat16 [16384, 2048], P(('fsdp', 'ctx', 'tensor'))
- attn_gain_grad: float32 [2048], P(('fsdp', 'ctx', 'tensor'))
- query_grad: float32 [2048, 2048], P(('fsdp', 'ctx'), 'tensor')
- key_grad: float32 [2048, 2048], P(('fsdp', 'ctx'), 'tensor')
- value_grad: float32 [2048, 2048], P(('fsdp', 'ctx'), 'tensor')
- output_grad: float32 [2048, 2048], P(('fsdp', 'ctx'), 'tensor')
- mlp_gain_grad: float32 [2048], P(('fsdp', 'ctx', 'tensor'))
- gate_grad: float32 [2048, 8192], P(('fsdp', 'ctx'), 'tensor')
- up_grad: float32 [2048, 8192], P(('fsdp', 'ctx'), 'tensor')
- down_grad: float32 [2048, 8192], P(('fsdp', 'ctx'), 'tensor')
Inputs may be any that keep to these rules, and one draw needn't show every extreme that they name: `seg_lengths`: row t gives the token counts of tree t's 4 branches and then its 16 leaves, which follow its trunk of 2176 tokens in this order; each row sums to 1920 and its largest entry is 128. `leaf_parent`: the branch, numbered 1 to 4, that each leaf hangs from.
All inputs are finite; a program needn't handle non-finite values.
Results may differ from a plain program's by a relative error of at most 0.02.
Values may be sent and summed in bfloat16 or wider, within the bound.
A program may use at most 448 MiB of HBM per device.

v0:
```python
import jax
import jax.numpy as jnp
from jax import lax
from jax.sharding import PartitionSpec as P

HEAD_DIM = 64
TRUNK = 2176
ROPE_BASE = 130000.0
EPSILON = 1e-05
NEG_LARGE = -1e30


def pick_table(onehot, table):
    return jnp.sum(jnp.where(onehot, table[None, :], 0), axis=1)


def tree_tables(lengths_row, parent_row, tree_len):
    branches = lengths_row.shape[0] - parent_row.shape[0]
    ends = TRUNK + jnp.cumsum(lengths_row)
    starts = ends - lengths_row
    matches = parent_row[:, None] - 1 == jnp.arange(branches, dtype=jnp.int32)[None, :]
    parent_len = jnp.sum(jnp.where(matches, lengths_row[None, :branches], 0), axis=1)
    zero_one = jnp.zeros((1,), jnp.int32)
    seg_start = jnp.concatenate([zero_one, starts])
    seg_base = jnp.concatenate(
        [zero_one, jnp.full((branches,), TRUNK, jnp.int32), TRUNK + parent_len]
    )
    seg_parent = jnp.concatenate([zero_one, jnp.zeros((branches,), jnp.int32), parent_row])
    positions = jnp.arange(tree_len, dtype=jnp.int32)
    above = jnp.sum((ends[None, :] <= positions[:, None]).astype(jnp.int32), axis=1)
    segment = (positions >= TRUNK).astype(jnp.int32) + above
    onehot = segment[:, None] == jnp.arange(seg_start.shape[0], dtype=jnp.int32)[None, :]
    depth = positions - pick_table(onehot, seg_start) + pick_table(onehot, seg_base)
    parent = pick_table(onehot, seg_parent)
    return (segment, parent, depth)


def rotate(values, depth, sign):
    count = values.shape[0]
    width = values.shape[1]
    heads = width // HEAD_DIM
    half = HEAD_DIM // 2
    freqs = jnp.power(ROPE_BASE, -(2.0 * jnp.arange(half, dtype=jnp.float32)) / HEAD_DIM)
    angles = depth.astype(jnp.float32)[:, None] * freqs[None, :]
    cosine = jnp.cos(angles)[:, None, :]
    sine = sign * jnp.sin(angles)[:, None, :]
    shaped = values.reshape(count, heads, HEAD_DIM)
    first = shaped[..., :half]
    second = shaped[..., half:]
    turned = jnp.concatenate(
        [first * cosine - second * sine, second * cosine + first * sine], axis=-1
    )
    return turned.reshape(count, width)


def normalize(rows):
    norm_inv = lax.rsqrt(jnp.mean(rows * rows, axis=1, keepdims=True) + EPSILON)
    return (rows * norm_inv, norm_inv)


def norm_backward(grad_rows, scaled, norm_inv, gain):
    weighted = grad_rows * gain[None, :]
    inner = jnp.mean(weighted * scaled, axis=1, keepdims=True)
    return (norm_inv * (weighted - scaled * inner), jnp.sum(grad_rows * scaled, axis=0))


def spread_rows(rows):
    return lax.all_gather(rows, "tensor", axis=0, tiled=True)


def reduce_rows(rows):
    return lax.psum_scatter(rows, "tensor", scatter_dimension=0, tiled=True)


def contract_first(left, right):
    return lax.dot_general(
        left, right, (((0,), (0,)), ((), ())), preferred_element_type=jnp.float32
    )


def contract_last(left, right):
    return lax.dot_general(
        left, right, (((1,), (1,)), ((), ())), preferred_element_type=jnp.float32
    )


def body(
    tokens_in,
    attn_gain,
    query_weight,
    key_weight,
    value_weight,
    output_weight,
    mlp_gain,
    gate_weight,
    up_weight,
    down_weight,
    seg_lengths,
    leaf_parent,
    cotangent,
):
    local_rows = tokens_in.shape[0]
    piece = local_rows * lax.axis_size("tensor")
    blocks = lax.axis_size("ctx")
    tree_len = piece * blocks
    score_scale = HEAD_DIM ** (-0.5)
    segment, parent, depth = tree_tables(seg_lengths[0], leaf_parent[0], tree_len)
    first_row = lax.axis_index("ctx") * piece
    query_seg = lax.dynamic_slice_in_dim(segment, first_row, piece)
    query_par = lax.dynamic_slice_in_dim(parent, first_row, piece)
    query_depth = lax.dynamic_slice_in_dim(depth, first_row, piece)
    query_index = first_row + jnp.arange(piece, dtype=jnp.int32)
    key_seg = segment.reshape(blocks, piece)
    key_index = jnp.arange(tree_len, dtype=jnp.int32).reshape(blocks, piece)
    wq_full, wk_full, wv_full, wo_full = (
        lax.all_gather(query_weight, "fsdp", axis=0, tiled=True),
        lax.all_gather(key_weight, "fsdp", axis=0, tiled=True),
        lax.all_gather(value_weight, "fsdp", axis=0, tiled=True),
        lax.all_gather(output_weight, "fsdp", axis=0, tiled=True),
    )
    wg_full, wu_full, wd_full = (
        lax.all_gather(gate_weight, "fsdp", axis=0, tiled=True),
        lax.all_gather(up_weight, "fsdp", axis=0, tiled=True),
        lax.all_gather(down_weight, "fsdp", axis=0, tiled=True),
    )
    x_rows = tokens_in.astype(jnp.float32)
    attn_scaled, attn_inv = normalize(x_rows)
    attn_in = spread_rows((attn_scaled * attn_gain[None, :]).astype(jnp.bfloat16))
    query_pre = jnp.dot(attn_in, wq_full, preferred_element_type=jnp.float32)
    key_pre = jnp.dot(attn_in, wk_full, preferred_element_type=jnp.float32)
    value_pre = jnp.dot(attn_in, wv_full, preferred_element_type=jnp.float32)
    query_rows = rotate(query_pre, query_depth, 1.0).astype(jnp.bfloat16)
    key_rows = rotate(key_pre, query_depth, 1.0).astype(jnp.bfloat16)
    value_rows = value_pre.astype(jnp.bfloat16)
    key_all, value_all = (
        lax.all_gather(key_rows, "ctx", axis=0, tiled=True),
        lax.all_gather(value_rows, "ctx", axis=0, tiled=True),
    )
    width = query_rows.shape[1]
    heads = width // HEAD_DIM
    query_heads = query_rows.reshape(piece, heads, HEAD_DIM)
    key_blocks = key_all.reshape(blocks, piece, heads, HEAD_DIM)
    value_blocks = value_all.reshape(blocks, piece, heads, HEAD_DIM)

    def block_scores(key_block, seg_block, index_block):
        raw = (
            jnp.einsum("qhd,khd->hqk", query_heads, key_block, preferred_element_type=jnp.float32)
            * score_scale
        )
        seen = (
            (seg_block[None, :] == query_seg[:, None])
            | (seg_block[None, :] == 0)
            | (seg_block[None, :] == query_par[:, None])
        ) & (index_block[None, :] <= query_index[:, None])
        return jnp.where(seen[None], raw, NEG_LARGE)

    def total_step(running, inputs):
        largest, total = running
        key_block, seg_block, index_block = inputs
        scores = block_scores(key_block, seg_block, index_block)
        newest = jnp.maximum(largest, jnp.max(scores, axis=2, keepdims=True))
        total = total * jnp.exp(largest - newest) + jnp.sum(
            jnp.exp(scores - newest), axis=2, keepdims=True
        )
        return ((newest, total), None)

    start_max = jnp.full((heads, piece, 1), NEG_LARGE, jnp.float32)
    start_total = jnp.zeros((heads, piece, 1), jnp.float32)
    (largest, total), unused = lax.scan(
        total_step, (start_max, start_total), (key_blocks, key_seg, key_index)
    )
    log_total = largest + jnp.log(total)

    def output_step(weighted, inputs):
        key_block, value_block, seg_block, index_block = inputs
        probs = jnp.exp(block_scores(key_block, seg_block, index_block) - log_total).astype(
            jnp.bfloat16
        )
        return (
            weighted
            + jnp.einsum("hqk,khd->qhd", probs, value_block, preferred_element_type=jnp.float32),
            None,
        )

    key_inputs = (key_blocks, value_blocks, key_seg, key_index)
    weighted, unused = lax.scan(
        output_step, jnp.zeros((piece, heads, HEAD_DIM), jnp.float32), key_inputs
    )
    attn_out = weighted.reshape(piece, width).astype(jnp.bfloat16)
    mid_rows = x_rows + reduce_rows(contract_last(attn_out, wo_full))
    mlp_scaled, mlp_inv = normalize(mid_rows)
    mlp_in = spread_rows((mlp_scaled * mlp_gain[None, :]).astype(jnp.bfloat16))
    gate = jnp.dot(mlp_in, wg_full, preferred_element_type=jnp.float32)
    up_proj = jnp.dot(mlp_in, wu_full, preferred_element_type=jnp.float32)
    hidden = (jax.nn.silu(gate) * up_proj).astype(jnp.bfloat16)
    final_rows = mid_rows + reduce_rows(contract_last(hidden, wd_full))
    block_out = final_rows.astype(jnp.bfloat16)
    out_grad_all = spread_rows(cotangent)
    down_grad = contract_first(out_grad_all, hidden)
    hidden_grad = jnp.dot(out_grad_all, wd_full, preferred_element_type=jnp.float32)
    sigmoid_gate = jax.nn.sigmoid(gate)
    gate_rows_grad = (
        hidden_grad * up_proj * sigmoid_gate * (1.0 + gate * (1.0 - sigmoid_gate))
    ).astype(jnp.bfloat16)
    up_rows_grad = (hidden_grad * gate * sigmoid_gate).astype(jnp.bfloat16)
    gate_grad = contract_first(mlp_in, gate_rows_grad)
    up_grad = contract_first(mlp_in, up_rows_grad)
    mlp_in_grad = reduce_rows(
        contract_last(gate_rows_grad, wg_full) + contract_last(up_rows_grad, wu_full)
    )
    mlp_back, mlp_gain_part = norm_backward(mlp_in_grad, mlp_scaled, mlp_inv, mlp_gain)
    mid_grad = cotangent.astype(jnp.float32) + mlp_back
    mid_all = spread_rows(mid_grad.astype(jnp.bfloat16))
    output_grad = contract_first(mid_all, attn_out)
    out_heads_grad = (
        jnp.dot(mid_all, wo_full, preferred_element_type=jnp.float32)
        .astype(jnp.bfloat16)
        .reshape(piece, heads, HEAD_DIM)
    )

    def delta_step(delta, inputs):
        key_block, value_block, seg_block, index_block = inputs
        attn_prob = jnp.exp(block_scores(key_block, seg_block, index_block) - log_total)
        prob_grad = jnp.einsum(
            "qhd,khd->hqk", out_heads_grad, value_block, preferred_element_type=jnp.float32
        )
        return (delta + jnp.sum(attn_prob * prob_grad, axis=2, keepdims=True), None)

    delta, unused = lax.scan(delta_step, jnp.zeros((heads, piece, 1), jnp.float32), key_inputs)

    def grad_step(query_total, inputs):
        key_block, value_block, seg_block, index_block = inputs
        attn_prob = jnp.exp(block_scores(key_block, seg_block, index_block) - log_total)
        prob_grad = jnp.einsum(
            "qhd,khd->hqk", out_heads_grad, value_block, preferred_element_type=jnp.float32
        )
        score_grad = (attn_prob * (prob_grad - delta)).astype(jnp.bfloat16)
        query_total = (
            query_total
            + jnp.einsum("hqk,khd->qhd", score_grad, key_block, preferred_element_type=jnp.float32)
            * score_scale
        )
        key_part = (
            jnp.einsum("hqk,qhd->khd", score_grad, query_heads, preferred_element_type=jnp.float32)
            * score_scale
        )
        value_part = jnp.einsum(
            "hqk,qhd->khd",
            attn_prob.astype(jnp.bfloat16),
            out_heads_grad,
            preferred_element_type=jnp.float32,
        )
        return (query_total, (key_part, value_part))

    query_sum, (key_parts, value_parts) = lax.scan(
        grad_step, jnp.zeros((piece, heads, HEAD_DIM), jnp.float32), key_inputs
    )
    key_sum, value_sum = (
        lax.psum_scatter(
            key_parts.reshape(tree_len, width).astype(jnp.bfloat16),
            "ctx",
            scatter_dimension=0,
            tiled=True,
        ).astype(jnp.float32),
        lax.psum_scatter(
            value_parts.reshape(tree_len, width).astype(jnp.bfloat16),
            "ctx",
            scatter_dimension=0,
            tiled=True,
        ).astype(jnp.float32),
    )
    query_pre_grad = rotate(query_sum.reshape(piece, width), query_depth, -1.0).astype(jnp.bfloat16)
    key_pre_grad = rotate(key_sum, query_depth, -1.0).astype(jnp.bfloat16)
    value_pre_grad = value_sum.astype(jnp.bfloat16)
    query_grad = contract_first(attn_in, query_pre_grad)
    key_grad = contract_first(attn_in, key_pre_grad)
    value_grad = contract_first(attn_in, value_pre_grad)
    attn_in_grad = reduce_rows(
        contract_last(query_pre_grad, wq_full)
        + contract_last(key_pre_grad, wk_full)
        + contract_last(value_pre_grad, wv_full)
    )
    attn_back, attn_gain_part = norm_backward(attn_in_grad, attn_scaled, attn_inv, attn_gain)
    input_grad = (mid_grad + attn_back).astype(jnp.bfloat16)
    attn_gain_grad, mlp_gain_grad = (
        lax.psum_scatter(
            attn_gain_part, ("fsdp", "ctx", "tensor"), scatter_dimension=0, tiled=True
        ),
        lax.psum_scatter(mlp_gain_part, ("fsdp", "ctx", "tensor"), scatter_dimension=0, tiled=True),
    )
    query_out, key_out, value_out, output_out, gate_out, up_out, down_out = (
        lax.psum_scatter(
            query_grad.astype(jnp.bfloat16), ("fsdp", "ctx"), scatter_dimension=0, tiled=True
        ).astype(jnp.float32),
        lax.psum_scatter(
            key_grad.astype(jnp.bfloat16), ("fsdp", "ctx"), scatter_dimension=0, tiled=True
        ).astype(jnp.float32),
        lax.psum_scatter(
            value_grad.astype(jnp.bfloat16), ("fsdp", "ctx"), scatter_dimension=0, tiled=True
        ).astype(jnp.float32),
        lax.psum_scatter(
            output_grad.astype(jnp.bfloat16), ("fsdp", "ctx"), scatter_dimension=0, tiled=True
        ).astype(jnp.float32),
        lax.psum_scatter(
            gate_grad.astype(jnp.bfloat16), ("fsdp", "ctx"), scatter_dimension=0, tiled=True
        ).astype(jnp.float32),
        lax.psum_scatter(
            up_grad.astype(jnp.bfloat16), ("fsdp", "ctx"), scatter_dimension=0, tiled=True
        ).astype(jnp.float32),
        lax.psum_scatter(
            down_grad.astype(jnp.bfloat16), ("fsdp", "ctx"), scatter_dimension=0, tiled=True
        ).astype(jnp.float32),
    )
    return (
        block_out,
        input_grad,
        attn_gain_grad,
        query_out,
        key_out,
        value_out,
        output_out,
        mlp_gain_grad,
        gate_out,
        up_out,
        down_out,
    )


def solution(mesh):
    in_specs = (
        P(("fsdp", "ctx", "tensor"), None),
        P(),
        P("fsdp", "tensor"),
        P("fsdp", "tensor"),
        P("fsdp", "tensor"),
        P("fsdp", "tensor"),
        P(),
        P("fsdp", "tensor"),
        P("fsdp", "tensor"),
        P("fsdp", "tensor"),
        P("fsdp", None),
        P("fsdp", None),
        P(("fsdp", "ctx", "tensor"), None),
    )
    out_specs = (
        P(("fsdp", "ctx", "tensor"), None),
        P(("fsdp", "ctx", "tensor"), None),
        P(("fsdp", "ctx", "tensor")),
        P(("fsdp", "ctx"), "tensor"),
        P(("fsdp", "ctx"), "tensor"),
        P(("fsdp", "ctx"), "tensor"),
        P(("fsdp", "ctx"), "tensor"),
        P(("fsdp", "ctx", "tensor")),
        P(("fsdp", "ctx"), "tensor"),
        P(("fsdp", "ctx"), "tensor"),
        P(("fsdp", "ctx"), "tensor"),
    )
    return jax.shard_map(body, mesh=mesh, in_specs=in_specs, out_specs=out_specs, check_vma=False)
```

profile of v0, /device:TPU:0, one launch (start us, length us, event | category | flops | bytes accessed | tf_op | source)
XLA Modules:
  0.0 4075.0 jit_solution(14927405452069166986)
XLA Ops:
  17.7 55.3 %all-gather.14.cloned.1.call-done = bf16[1024,2048]{1,0:T(8,128)(2,1)} async-done(((bf16[512,2048]{1,0:T(8,128)(2,1)}), bf16[1024,2048]{1,0:T(8,128)(2,1)}) %all-gather.14.cloned.1.call-update) | async-done | bytes 4194320 | tf_op jit(solution)/shard_map/all_gather | solution.py:68
  73.0 82.4 %all-gather.24.cloned.1.call-done = bf16[2048,1024]{1,0:T(8,128)(2,1)} async-done(((bf16[512,1024]{1,0:T(8,128)(2,1)}), bf16[2048,1024]{1,0:T(8,128)(2,1)}) %all-gather.24.cloned.1.call-update) | async-done | bytes 4194320 | tf_op jit(solution)/shard_map/all_gather | solution.py:116
  165.4 70.9 %all-gather.20.cloned.1.call-done = bf16[2048,1024]{1,0:T(8,128)(2,1)} async-done(((bf16[512,1024]{1,0:T(8,128)(2,1)}), bf16[2048,1024]{1,0:T(8,128)(2,1)}) %all-gather.20.cloned.1.call-update) | async-done | bytes 4194320 | tf_op jit(solution)/shard_map/all_gather | solution.py:117
  248.3 68.8 %all-gather.16.cloned.1.call-done = bf16[2048,1024]{1,0:T(8,128)(2,1)} async-done(((bf16[512,1024]{1,0:T(8,128)(2,1)}), bf16[2048,1024]{1,0:T(8,128)(2,1)}) %all-gather.16.cloned.1.call-update) | async-done | bytes 4194320 | tf_op jit(solution)/shard_map/all_gather | solution.py:118
  328.8 47.1 %all-gather.22.cloned.1.call-done = bf16[4096,1024]{0,1:T(8,128)(2,1)} async-done(((bf16[1024,1024]{0,1:T(8,128)(2,1)}), bf16[4096,1024]{0,1:T(8,128)(2,1)}) %all-gather.22.cloned.1.call-update) | async-done | bytes 8388624 | tf_op jit(solution)/shard_map/all_gather | solution.py:136
  400.2 197.2 %while.50 = (s32[]{:T(128)}, f32[16,1024,1]{1,0,2:T(8,128)S(1)}, f32[16,1024,1]{1,0,2:T(8,128)S(1)}, s32[4,1024]{1,0:T(4,128)S(1)}, s32[1024]{0:T(1024)S(1)}, /*...) while((s32[]{:T(128)}, f32[16,1024,1]{1,0,2:T(8,128)S(1)}, ...), condition=%wide.region_10.11_spmd.clone, body=%wide.region_7.10_spmd.clone.sunk | while | flops 2271299584 | bytes 142452880 | solution.py:169
  637.9 109.1 %while.51 = (s32[]{:T(128)}, f32[1024,16,64]{0,2,1:T(8,128)}, bf16[4,1024,16,64]{1,3,2,0:T(8,128)(2,1)}, s32[4,1024]{1,0:T(4,128)S(1)}, s32[1024]{0:T(1024)S(1)}...) while((s32[]{:T(128)}, f32[1024,16,64]{0,2,1:T(8,128)}, ...), condition=%wide.region_12.13_spmd.clone, body=%wide.region_11.12_spmd.clone.sunk | while | flops 4370466816 | bytes 16887448 | solution.py:186
  763.2 98.6 %reduce-scatter.16.cloned.1.call-done = f32[512,2048]{1,0:T(8,128)} async-done(((f32[1024,2048]{1,0:T(8,128)}), f32[512,2048]{1,0:T(8,128)}) %reduce-scatter.16.cloned.1.call-update) | async-done | bytes 4194320 | tf_op jit(solution)/shard_map/reduce_scatter | solution.py:72
  870.4 279.8 %all-gather.32.cloned.1.call-done = bf16[2048,4096]{1,0:T(8,128)(2,1)} async-done(((bf16[512,4096]{1,0:T(8,128)(2,1)}), bf16[2048,4096]{1,0:T(8,128)(2,1)}) %all-gather.32.cloned.1.call-update) | async-done | bytes 16777232 | tf_op jit(solution)/shard_map/all_gather | solution.py:123
  1150.2 57.0 %all-gather.28.cloned.1.call-done = bf16[1024,2048]{1,0:T(8,128)(2,1)} async-done(((bf16[512,2048]{1,0:T(8,128)(2,1)}), bf16[1024,2048]{1,0:T(8,128)(2,1)}) %all-gather.28.cloned.1.call-update) | async-done | bytes 4194320 | tf_op jit(solution)/shard_map/all_gather | solution.py:68
  1230.6 265.0 %all-gather.30.cloned.1.call-done = bf16[2048,4096]{1,0:T(8,128)(2,1)} async-done(((bf16[512,4096]{1,0:T(8,128)(2,1)}), bf16[2048,4096]{1,0:T(8,128)(2,1)}) %all-gather.30.cloned.1.call-update) | async-done | bytes 16777232 | tf_op jit(solution)/shard_map/all_gather | solution.py:122
  1519.1 33.0 all-gather.36.cloned.1.call-done
  1552.1 288.5 %all-gather.34.cloned.1.call-done = bf16[2048,4096]{1,0:T(8,128)(2,1)} async-done(((bf16[512,4096]{1,0:T(8,128)(2,1)}), bf16[2048,4096]{1,0:T(8,128)(2,1)}) %all-gather.34.cloned.1.call-update) | async-done | bytes 16777232 | tf_op jit(solution)/shard_map/all_gather | solution.py:124
  1840.6 34.7 multiply_convert_fusion
  1919.1 97.5 %reduce-scatter.20.cloned.1.call-done = f32[512,2048]{1,0:T(8,128)} async-done(((f32[1024,2048]{1,0:T(8,128)}), f32[512,2048]{1,0:T(8,128)}) %reduce-scatter.20.cloned.1.call-update) | async-done | bytes 4194320 | tf_op jit(solution)/shard_map/reduce_scatter | solution.py:72
  2025.7 56.3 %all-gather.38.cloned.1.call-done = bf16[1024,2048]{1,0:T(8,128)(2,1)} async-done(((bf16[512,2048]{1,0:T(8,128)(2,1)}), bf16[1024,2048]{1,0:T(8,128)(2,1)}) %all-gather.38.cloned.1.call-update) | async-done | bytes 4194320 | tf_op jit(solution)/shard_map/all_gather | solution.py:68
  2091.4 223.1 %while.52 = (s32[]{:T(128)}, f32[16,1024,1]{1,2,0:T(1,128)S(1)}, s32[4,1024]{1,0:T(4,128)S(1)}, s32[1024]{0:T(1024)S(1)}, s32[1024]{0:T(1024)S(1)}, /*index=5*/s...) while((s32[]{:T(128)}, f32[16,1024,1]{1,2,0:T(1,128)S(1)}, ...), condition=%wide.region_20.21_spmd.clone, body=%wide.region_18.20_spmd.clone.sunk | while | flops 4385163264 | bytes 145074336 | solution.py:229
  2314.5 522.7 %while.53 = (s32[]{:T(128)}, f32[1024,16,64]{0,2,1:T(8,128)}, bf16[4,1024,16,64]{1,3,2,0:T(8,128)(2,1)}, bf16[4,1024,16,64]{1,3,2,0:T(8,128)(2,1)}, bf16[4,1024,...) while((s32[]{:T(128)}, f32[1024,16,64]{0,2,1:T(8,128)}, ...), condition=%wide.region_22.23_spmd.clone, body=%wide.region_21.22_spmd.clone.sunk | while | flops 10915678208 | bytes 336832672 | solution.py:255
  2367.5 41.2 %fusion.197 = bf16[16,1024,1024]{1,2,0:T(8,128)(2,1)} fusion(f32[16,1024,1024]{2,1,0:T(8,128)} %fusion.196, f32[16,1024]{1,0:T(8,128)S(1)} %bitcast.308, f32[16,1024]{1,0:T(8,128)S(1)} %bitcast.307, pred[1024,1024]{0,1:T(8,128)(4,1)S(1)} %compare_and_fusion.11, bf16[1024,16,64]{0,2,1:T(8,128)(2,1)} %get-tuple-element.1279, ...), kind=kOutput, calls=%fused_computation.59.clone.2 | convolution fusion | flops 2248146944 | bytes 106037248 | tf_op jit(solution)/shard_map/while/body/eval_jaxpr/qhd,khd->hqk/dot_general | solution.py:234
  2497.1 41.2 %fusion.197 = bf16[16,1024,1024]{1,2,0:T(8,128)(2,1)} fusion(f32[16,1024,1024]{2,1,0:T(8,128)} %fusion.196, f32[16,1024]{1,0:T(8,128)S(1)} %bitcast.308, f32[16,1024]{1,0:T(8,128)S(1)} %bitcast.307, pred[1024,1024]{0,1:T(8,128)(4,1)S(1)} %compare_and_fusion.11, bf16[1024,16,64]{0,2,1:T(8,128)(2,1)} %get-tuple-element.1279, ...), kind=kOutput, calls=%fused_computation.59.clone.2 | convolution fusion | flops 2248146944 | bytes 106037248 | tf_op jit(solution)/shard_map/while/body/eval_jaxpr/qhd,khd->hqk/dot_general | solution.py:234
  2628.0 41.2 %fusion.197 = bf16[16,1024,1024]{1,2,0:T(8,128)(2,1)} fusion(f32[16,1024,1024]{2,1,0:T(8,128)} %fusion.196, f32[16,1024]{1,0:T(8,128)S(1)} %bitcast.308, f32[16,1024]{1,0:T(8,128)S(1)} %bitcast.307, pred[1024,1024]{0,1:T(8,128)(4,1)S(1)} %compare_and_fusion.11, bf16[1024,16,64]{0,2,1:T(8,128)(2,1)} %get-tuple-element.1279, ...), kind=kOutput, calls=%fused_computation.59.clone.2 | convolution fusion | flops 2248146944 | bytes 106037248 | tf_op jit(solution)/shard_map/while/body/eval_jaxpr/qhd,khd->hqk/dot_general | solution.py:234
  2758.8 41.2 %fusion.197 = bf16[16,1024,1024]{1,2,0:T(8,128)(2,1)} fusion(f32[16,1024,1024]{2,1,0:T(8,128)} %fusion.196, f32[16,1024]{1,0:T(8,128)S(1)} %bitcast.308, f32[16,1024]{1,0:T(8,128)S(1)} %bitcast.307, pred[1024,1024]{0,1:T(8,128)(4,1)S(1)} %compare_and_fusion.11, bf16[1024,16,64]{0,2,1:T(8,128)(2,1)} %get-tuple-element.1279, ...), kind=kOutput, calls=%fused_computation.59.clone.2 | convolution fusion | flops 2248146944 | bytes 106037248 | tf_op jit(solution)/shard_map/while/body/eval_jaxpr/qhd,khd->hqk/dot_general | solution.py:234
  3084.9 104.4 %reduce-scatter.40.cloned.1.call-done = bf16[128,4096]{1,0:T(8,128)(2,1)} async-done(((bf16[2048,4096]{1,0:T(8,128)(2,1)}), bf16[128,4096]{1,0:T(8,128)(2,1)}) %reduce-scatter.40.cloned.1.call-update) | async-done | bytes 1048592
  3192.5 178.4 %reduce-scatter.38.cloned.1.call-done = bf16[128,4096]{1,0:T(8,128)(2,1)} async-done(((bf16[2048,4096]{1,0:T(8,128)(2,1)}), bf16[128,4096]{1,0:T(8,128)(2,1)}) %reduce-scatter.38.cloned.1.call-update) | async-done | bytes 1048592 | tf_op jit(solution)/shard_map/reduce_scatter | solution.py:307
  3373.7 178.8 %reduce-scatter.36.cloned.1.call-done = bf16[128,4096]{1,0:T(8,128)(2,1)} async-done(((bf16[2048,4096]{1,0:T(8,128)(2,1)}), bf16[128,4096]{1,0:T(8,128)(2,1)}) %reduce-scatter.36.cloned.1.call-update) | async-done | bytes 1048592 | tf_op jit(solution)/shard_map/reduce_scatter | solution.py:304
  3555.2 72.5 %reduce-scatter.34.cloned.1.call-done = bf16[128,1024]{1,0:T(8,128)(2,1)} async-done(((bf16[2048,1024]{1,0:T(8,128)(2,1)}), bf16[128,1024]{1,0:T(8,128)(2,1)}) %reduce-scatter.34.cloned.1.call-update) | async-done | bytes 262160 | tf_op jit(solution)/shard_map/reduce_scatter | solution.py:301
  3629.5 74.1 %reduce-scatter.32.cloned.1.call-done = bf16[128,1024]{1,0:T(8,128)(2,1)} async-done(((bf16[2048,1024]{1,0:T(8,128)(2,1)}), bf16[128,1024]{1,0:T(8,128)(2,1)}) %reduce-scatter.32.cloned.1.call-update) | async-done | bytes 262160 | tf_op jit(solution)/shard_map/reduce_scatter | solution.py:298
  3705.4 73.8 %reduce-scatter.28.cloned.1.call-done = bf16[128,1024]{1,0:T(8,128)(2,1)} async-done(((bf16[2048,1024]{1,0:T(8,128)(2,1)}), bf16[128,1024]{1,0:T(8,128)(2,1)}) %reduce-scatter.28.cloned.1.call-update) | async-done | bytes 262160 | tf_op jit(solution)/shard_map/reduce_scatter | solution.py:292
  3780.9 73.8 %reduce-scatter.30.cloned.1.call-done = bf16[128,1024]{1,0:T(8,128)(2,1)} async-done(((bf16[2048,1024]{1,0:T(8,128)(2,1)}), bf16[128,1024]{1,0:T(8,128)(2,1)}) %reduce-scatter.30.cloned.1.call-update) | async-done | bytes 262160 | tf_op jit(solution)/shard_map/reduce_scatter | solution.py:295
  3856.6 98.9 %reduce-scatter.26.cloned.1.call-done = f32[512,2048]{1,0:T(8,128)} async-done(((f32[1024,2048]{1,0:T(8,128)}), f32[512,2048]{1,0:T(8,128)}) %reduce-scatter.26.cloned.1.call-update) | async-done | bytes 4194320 | tf_op jit(solution)/shard_map/reduce_scatter | solution.py:72
  3958.8 40.0 all-reduce.2
  4000.0 58.3 %reduce-scatter.18.cloned.1.call-done = f32[512,2048]{1,0:T(8,128)} async-done(((f32[1024,2048]{1,0:T(8,128)}), f32[512,2048]{1,0:T(8,128)}) %reduce-scatter.18.cloned.1.call-update) | async-done | bytes 4194320 | tf_op jit(solution)/shard_map/reduce_scatter | solution.py:72
  (359 shorter events, 1405.6 us)
Async XLA Ops:
  7.2 65.8 %all-gather.14.cloned.1.call-start = ((), (), s32[]{:S(2)}) async-start(), calls=%async_computation.13 | async-start | bytes 6291456 | tf_op jit(solution)/shard_map/all_gather | solution.py:68
  13.4 142.0 %all-gather.24.cloned.1.call-start = ((), (), s32[]{:S(2)}) async-start(), calls=%async_computation.18 | async-start | bytes 5242880 | tf_op jit(solution)/shard_map/all_gather | solution.py:116
  14.2 222.1 %all-gather.20.cloned.1.call-start = ((), (), s32[]{:S(2)}) async-start(), calls=%async_computation.16 | async-start | bytes 5242880 | tf_op jit(solution)/shard_map/all_gather | solution.py:117
  14.9 302.1 %all-gather.16.cloned.1.call-start = ((), (), s32[]{:S(2)}) async-start(), calls=%async_computation.14 | async-start | bytes 5242880 | tf_op jit(solution)/shard_map/all_gather | solution.py:118
  15.5 360.4 %all-gather.22.cloned.1.call-start = ((), (), s32[]{:S(2)}) async-start(), calls=%async_computation.17 | async-start | bytes 10485760 | tf_op jit(solution)/shard_map/all_gather | solution.py:136
  248.0 349.4 %all-gather.18.cloned.1.call-start = ((), (), s32[]{:S(2)}) async-start(), calls=%async_computation.15 | async-start | bytes 10485760 | tf_op jit(solution)/shard_map/all_gather | solution.py:137
  326.3 425.3 %all-gather.26.cloned.1.call-start = ((), (), s32[]{:S(2)}) async-start(), calls=%async_computation.19 | async-start | bytes 5242880 | tf_op jit(solution)/shard_map/all_gather | solution.py:119
  327.1 534.6 %reduce-scatter.16.cloned.1.call-start = ((), (), s32[]{:S(2)}) async-start(), calls=%async_computation.20 | async-start | bytes 12582912 | tf_op jit(solution)/shard_map/reduce_scatter | solution.py:72
  762.4 387.8 %all-gather.32.cloned.1.call-start = ((), (), s32[]{:S(2)}) async-start(), calls=%async_computation.23 | async-start | bytes 20971520 | tf_op jit(solution)/shard_map/all_gather | solution.py:123
  763.1 444.1 %all-gather.28.cloned.1.call-start = ((), (), s32[]{:S(2)}) async-start(), calls=%async_computation.21 | async-start | bytes 6291456 | tf_op jit(solution)/shard_map/all_gather | solution.py:68
  868.3 627.4 %all-gather.30.cloned.1.call-start = ((), (), s32[]{:S(2)}) async-start(), calls=%async_computation.22 | async-start | bytes 20971520 | tf_op jit(solution)/shard_map/all_gather | solution.py:122
  869.0 683.1 %all-gather.36.cloned.1.call-start = ((), (), s32[]{:S(2)}) async-start(), calls=%async_computation.26 | async-start | bytes 6291456 | tf_op jit(solution)/shard_map/all_gather | solution.py:68
  869.6 971.0 %all-gather.34.cloned.1.call-start = ((), (), s32[]{:S(2)}) async-start(), calls=%async_computation.24 | async-start | bytes 20971520 | tf_op jit(solution)/shard_map/all_gather | solution.py:124
  870.4 1146.3 %reduce-scatter.20.cloned.1.call-start = ((), (), s32[]{:S(2)}) async-start(), calls=%async_computation.27 | async-start | bytes 12582912 | tf_op jit(solution)/shard_map/reduce_scatter | solution.py:72
  1919.1 162.9 %all-gather.38.cloned.1.call-start = ((), (), s32[]{:S(2)}) async-start(), calls=%async_computation.28 | async-start | bytes 6291456 | tf_op jit(solution)/shard_map/all_gather | solution.py:68
  2025.1 967.3 %reduce-scatter.24.cloned.1.call-start = ((), (), s32[]{:S(2)}) async-start(), calls=%async_computation.30 | async-start | bytes 10485760 | tf_op jit(solution)/shard_map/reduce_scatter | solution.py:265
  2860.4 146.2 %reduce-scatter.22.cloned.1.call-start = ((), (), s32[]{:S(2)}) async-start(), calls=%async_computation.29 | async-start | bytes 10485760 | tf_op jit(solution)/shard_map/reduce_scatter | solution.py:259
  2885.5 303.8 %reduce-scatter.40.cloned.1.call-start = ((), (), s32[]{:S(2)}) async-start(), calls=%async_computation.38 | async-start | bytes 17825792
  2931.0 439.9 %reduce-scatter.38.cloned.1.call-start = ((), (), s32[]{:S(2)}) async-start(), calls=%async_computation.37 | async-start | bytes 17825792 | tf_op jit(solution)/shard_map/reduce_scatter | solution.py:307
  2956.0 596.4 %reduce-scatter.36.cloned.1.call-start = ((), (), s32[]{:S(2)}) async-start(), calls=%async_computation.36 | async-start | bytes 17825792 | tf_op jit(solution)/shard_map/reduce_scatter | solution.py:304
  2981.9 645.8 %reduce-scatter.34.cloned.1.call-start = ((), (), s32[]{:S(2)}) async-start(), calls=%async_computation.35 | async-start | bytes 4456448 | tf_op jit(solution)/shard_map/reduce_scatter | solution.py:301
  2992.1 711.5 %reduce-scatter.32.cloned.1.call-start = ((), (), s32[]{:S(2)}) async-start(), calls=%async_computation.34 | async-start | bytes 4456448 | tf_op jit(solution)/shard_map/reduce_scatter | solution.py:298
  3001.8 777.3 %reduce-scatter.28.cloned.1.call-start = ((), (), s32[]{:S(2)}) async-start(), calls=%async_computation.32 | async-start | bytes 4456448 | tf_op jit(solution)/shard_map/reduce_scatter | solution.py:292
  3020.3 834.4 %reduce-scatter.30.cloned.1.call-start = ((), (), s32[]{:S(2)}) async-start(), calls=%async_computation.33 | async-start | bytes 4456448 | tf_op jit(solution)/shard_map/reduce_scatter | solution.py:295
  3030.6 924.9 %reduce-scatter.26.cloned.1.call-start = ((), (), s32[]{:S(2)}) async-start(), calls=%async_computation.31 | async-start | bytes 12582912 | tf_op jit(solution)/shard_map/reduce_scatter | solution.py:72
  3060.3 998.0 %reduce-scatter.18.cloned.1.call-start = ((), (), s32[]{:S(2)}) async-start(), calls=%async_computation.25 | async-start | bytes 12582912 | tf_op jit(solution)/shard_map/reduce_scatter | solution.py:72
  3192.5 763.0 %copy-start.6 = (bf16[512,2048]{1,0:T(8,128)(2,1)S(1)}, bf16[512,2048]{1,0:T(8,128)(2,1)}, u32[]{:S(2)}) copy-start(bf16[512,2048]{1,0:T(8,128)(2,1)} %param.21) | copy-start | bytes 6291460
  3192.5 763.0 %copy-start.29 = (f32[2048]{0:T(1024)S(1)}, f32[2048]{0:T(1024)}, u32[]{:S(2)}) copy-start(f32[2048]{0:T(1024)} %param.22) | copy-start | bytes 24580
  3192.5 763.0 %copy-start.36 = (f32[512]{0:T(512)S(1)}, f32[512]{0:T(512)}, u32[]{:S(2)}) copy-start(f32[512]{0:T(512)} %copy-done.35) | copy-start | bytes 6148
  3629.5 428.8 %copy-start.28 = (f32[2048]{0:T(1024)S(1)}, f32[2048]{0:T(1024)}, u32[]{:S(2)}) copy-start(f32[2048]{0:T(1024)} %param.27) | copy-start | bytes 24580
  3629.5 428.8 %copy-start.34 = (f32[512]{0:T(512)S(1)}, f32[512]{0:T(512)}, u32[]{:S(2)}) copy-start(f32[512]{0:T(512)} %copy-done.32) | copy-start | bytes 6148
  3629.5 428.8 %copy-start.39 = (f32[512]{0:T(512)S(1)}, f32[512]{0:T(512)}, u32[]{:S(2)}) copy-start(f32[512]{0:T(512)} %copy-done.38) | copy-start | bytes 6148
  (43 other events, 1987.5 us)
Sparse Core Ops, SparseCore 0:
  13.5 59.4 all-gather.13
  74.6 80.7 all-gather.23
  157.0 79.2 all-gather.19
  237.7 79.2 all-gather.15
  319.0 56.8 all-gather.21
  377.9 58.2 all-gather.17
  437.7 80.7 all-gather.25
  762.5 99.2 reduce-scatter.15
  863.4 286.7 all-gather.31
  1152.2 54.9 all-gather.27
  1208.9 286.7 all-gather.29
  1497.1 54.9 all-gather.35
  1553.8 286.7 all-gather.33
  1919.2 97.4 reduce-scatter.19
  2025.2 56.7 all-gather.37
  2860.6 71.7 reduce-scatter.23
  2934.9 71.6 reduce-scatter.21
  3010.6 178.5 reduce-scatter.39
  3193.3 177.5 reduce-scatter.37
  3374.9 177.5 reduce-scatter.35
  3556.3 71.3 reduce-scatter.33
  3632.0 71.5 reduce-scatter.31
  3707.4 71.6 reduce-scatter.27
  3783.3 71.3 reduce-scatter.29
  3857.1 98.3 reduce-scatter.25
  3957.7 100.4 reduce-scatter.17
where the time goes:
time: 4090 us; the launch traced here: 4070 us
  waiting for transfers between devices  2420 us (59%)
  matrix products  1260 us (31%)
  other arithmetic  179 us (4%)
  local copies, waits for them, and re-layouts  150 us (4%)
    reduce_scatter x4, waiting for transfers between devices, reduce_rows(): return lax.psum_scatter(rows, 'tensor', scatter_dimension=0, tiled=True)  353 us
    dot_general x12, matrix products, block_scores(): jnp.einsum('qhd,khd->hqk', query_heads, key_block, preferred_element_type...  300 us
    all_gather x1, waiting for transfers between devices, body(): lax.all_gather(down_weight, 'fsdp', axis=0, tiled=True)  288 us
    all_gather x1, waiting for transfers between devices, body(): lax.all_gather(up_weight, 'fsdp', axis=0, tiled=True)  280 us
    all_gather x1, waiting for transfers between devices, body(): lax.all_gather(gate_weight, 'fsdp', axis=0, tiled=True)  265 us
    all_gather x4, waiting for transfers between devices, spread_rows(): return lax.all_gather(rows, 'tensor', axis=0, tiled=True)  202 us
    reduce_scatter x1, waiting for transfers between devices, body(): lax.psum_scatter(gate_grad.astype(jnp.bfloat16), ('fsdp', 'ctx'), scatter...  179 us
    reduce_scatter x1, waiting for transfers between devices, body(): lax.psum_scatter(up_grad.astype(jnp.bfloat16), ('fsdp', 'ctx'), scatter_d...  178 us
  transfers between devices with their start and end apart: 26, of which 23 were waited for; matrix products, arithmetic and copies ran while one was open for 17% of the time, Pallas kernels for 0%

commit v1 on v0

--- a/solution.py
+++ b/solution.py
@@ -8,6 +8,24 @@
 ROPE_BASE = 130000.0
 EPSILON = 1e-05
 NEG_LARGE = -1e30
+
+
+def ring_gather(shard, axis, dim):
+    ways, here, step = (lax.axis_size(axis), lax.axis_index(axis), shard.shape[dim])
+    dims = [n * ways if d == dim else n for d, n in enumerate(shard.shape)]
+    full = lax.dynamic_update_slice_in_dim(
+        jnp.zeros(dims, shard.dtype), shard, here * step, axis=dim
+    )
+    going_up = going_down = shard
+    for far in range(1, ways // 2 + 1):
+        going_up = lax.ppermute(going_up, axis, [(d, (d + 1) % ways) for d in range(ways)])
+        full = lax.dynamic_update_slice_in_dim(full, going_up, (here - far) % ways * step, axis=dim)
+        if 2 * far < ways:
+            going_down = lax.ppermute(going_down, axis, [(d, (d - 1) % ways) for d in range(ways)])
+            full = lax.dynamic_update_slice_in_dim(
+                full, going_down, (here + far) % ways * step, axis=dim
+            )
+    return full
 
 
 def pick_table(onehot, table):
@@ -119,7 +137,7 @@
         lax.all_gather(output_weight, "fsdp", axis=0, tiled=True),
     )
     wg_full, wu_full, wd_full = (
-        lax.all_gather(gate_weight, "fsdp", axis=0, tiled=True),
+        ring_gather(gate_weight, "fsdp", 0),
         lax.all_gather(up_weight, "fsdp", axis=0, tiled=True),
         lax.all_gather(down_weight, "fsdp", axis=0, tiled=True),
     )

time: 4090 us -> 3930 us (0.961)
  waiting for transfers between devices: 2420 us -> 2230 us
    ppermute x0 -> x3, waiting for transfers between devices: none -> 346 us  [the longest x2 243 us: ring_gather(): lax.ppermute(going_up, axis, [(d, (d + 1) % ways) for d in range(ways)])]
    all_gather x1 -> x0, waiting for transfers between devices: 265 us -> none  [body(): lax.all_gather(gate_weight, 'fsdp', axis=0, tiled=True)]
    all_gather x1, waiting for transfers between devices: 288 us -> 164 us  [body(): lax.all_gather(down_weight, 'fsdp', axis=0, tiled=True)]
    reduce_scatter x4, waiting for transfers between devices: 353 us -> 256 us  [reduce_rows(): return lax.psum_scatter(rows, 'tensor', scatter_dimension=0, tiled=True)]
    unnamed x27 -> x26, waiting for transfers between devices: 110 us -> 109 us
    unnamed x106 -> x110, local copies, waits for them, and re-layouts: 90.7 us -> 90.7 us
  transfers between devices with their start and end apart: 26 -> 28, of which waited for: 23 -> 23; matrix products, arithmetic and copies ran while one was open for 17% -> 18% of each run, Pallas kernels for 0% -> 0%
where the time goes in v1:
time: 3930 us; the launch traced here: 3920 us
  waiting for transfers between devices  2230 us (57%)
  matrix products  1270 us (32%)
  other arithmetic  179 us (5%)
  local copies, waits for them, and re-layouts  174 us (4%)
  blocking collectives  40.1 us (1%)
    dot_general x12, matrix products, block_scores(): jnp.einsum('qhd,khd->hqk', query_heads, key_block, preferred_element_type...  300 us
    all_gather x1, waiting for transfers between devices, body(): lax.all_gather(up_weight, 'fsdp', axis=0, tiled=True)  263 us
    reduce_scatter x4, waiting for transfers between devices, reduce_rows(): return lax.psum_scatter(rows, 'tensor', scatter_dimension=0, tiled=True)  256 us
    ppermute x2, waiting for transfers between devices, ring_gather(): lax.ppermute(going_up, axis, [(d, (d + 1) % ways) for d in range(ways)])  243 us
    reduce_scatter x1, waiting for transfers between devices, body(): lax.psum_scatter(up_grad.astype(jnp.bfloat16), ('fsdp', 'ctx'), scatter_d...  179 us
    reduce_scatter x1, waiting for transfers between devices, body(): lax.psum_scatter(gate_grad.astype(jnp.bfloat16), ('fsdp', 'ctx'), scatter...  178 us
    all_gather x4, waiting for transfers between devices, spread_rows(): return lax.all_gather(rows, 'tensor', axis=0, tiled=True)  169 us
    dot_general x4, matrix products, grad_step(): jnp.einsum('qhd,khd->hqk', out_heads_grad, value_block, preferred_element...  165 us
  transfers between devices with their start and end apart: 28, of which 23 were waited for; matrix products, arithmetic and copies ran while one was open for 18% of the time, Pallas kernels for 0%

profile of v1, /device:TPU:0, one launch (start us, length us, event | category | flops | bytes accessed | tf_op | source)
XLA Modules:
  0.0 3915.2 jit_solution(10396700462037421087)
XLA Ops:
  17.7 55.3 %all-gather.13.cloned.1.call-done = bf16[1024,2048]{1,0:T(8,128)(2,1)} async-done(((bf16[512,2048]{1,0:T(8,128)(2,1)}), bf16[1024,2048]{1,0:T(8,128)(2,1)}) %all-gather.13.cloned.1.call-update) | async-done | bytes 4194320 | tf_op jit(solution)/shard_map/all_gather | solution.py:86
  73.0 82.4 %all-gather.23.cloned.1.call-done = bf16[2048,1024]{1,0:T(8,128)(2,1)} async-done(((bf16[512,1024]{1,0:T(8,128)(2,1)}), bf16[2048,1024]{1,0:T(8,128)(2,1)}) %all-gather.23.cloned.1.call-update) | async-done | bytes 4194320 | tf_op jit(solution)/shard_map/all_gather | solution.py:134
  165.3 70.9 %all-gather.19.cloned.1.call-done = bf16[2048,1024]{1,0:T(8,128)(2,1)} async-done(((bf16[512,1024]{1,0:T(8,128)(2,1)}), bf16[2048,1024]{1,0:T(8,128)(2,1)}) %all-gather.19.cloned.1.call-update) | async-done | bytes 4194320 | tf_op jit(solution)/shard_map/all_gather | solution.py:135
  248.5 68.5 %all-gather.15.cloned.1.call-done = bf16[2048,1024]{1,0:T(8,128)(2,1)} async-done(((bf16[512,1024]{1,0:T(8,128)(2,1)}), bf16[2048,1024]{1,0:T(8,128)(2,1)}) %all-gather.15.cloned.1.call-update) | async-done | bytes 4194320 | tf_op jit(solution)/shard_map/all_gather | solution.py:136
  328.8 47.1 %all-gather.21.cloned.1.call-done = bf16[4096,1024]{0,1:T(8,128)(2,1)} async-done(((bf16[1024,1024]{0,1:T(8,128)(2,1)}), bf16[4096,1024]{0,1:T(8,128)(2,1)}) %all-gather.21.cloned.1.call-update) | async-done | bytes 8388624 | tf_op jit(solution)/shard_map/all_gather | solution.py:154
  400.2 197.1 %while.50 = (s32[]{:T(128)}, f32[16,1024,1]{1,0,2:T(8,128)S(1)}, f32[16,1024,1]{1,0,2:T(8,128)S(1)}, s32[4,1024]{1,0:T(4,128)S(1)}, s32[1024]{0:T(1024)S(1)}, /*...) while((s32[]{:T(128)}, f32[16,1024,1]{1,0,2:T(8,128)S(1)}, ...), condition=%wide.region_10.11_spmd.clone, body=%wide.region_7.10_spmd.clone.sunk | while | flops 2271299584 | bytes 142452880 | solution.py:187
  637.9 108.8 %while.51 = (s32[]{:T(128)}, f32[1024,16,64]{0,2,1:T(8,128)}, bf16[4,1024,16,64]{1,3,2,0:T(8,128)(2,1)}, s32[4,1024]{1,0:T(4,128)S(1)}, s32[1024]{0:T(1024)S(1)}...) while((s32[]{:T(128)}, f32[1024,16,64]{0,2,1:T(8,128)}, ...), condition=%wide.region_12.13_spmd.clone, body=%wide.region_11.12_spmd.clone.sunk | while | flops 4370466816 | bytes 16887448 | solution.py:204
  768.0 91.7 %collective-permute-done = bf16[512,4096]{1,0:T(8,128)(2,1)} collective-permute-done((bf16[512,4096]{1,0:T(8,128)(2,1)}, bf16[512,4096]{1,0:T(8,128)(2,1)}, u32[]{:S(2)}, u32[]{:S(2)}) %collective-permute-start) | collective-permute-done | bytes 4194336 | tf_op jit(solution)/shard_map/ppermute | solution.py:21
  881.1 103.8 %collective-permute-done.1 = bf16[512,4096]{1,0:T(8,128)(2,1)} collective-permute-done((bf16[512,4096]{1,0:T(8,128)(2,1)}, bf16[512,4096]{1,0:T(8,128)(2,1)}, u32[]{:S(2)}, u32[]{:S(2)}) %collective-permute-start.1) | collective-permute-done | bytes 4194336 | tf_op jit(solution)/shard_map/ppermute | solution.py:24
  989.7 150.8 %collective-permute-done.2 = bf16[512,4096]{1,0:T(8,128)(2,1)} collective-permute-done((bf16[512,4096]{1,0:T(8,128)(2,1)}, bf16[512,4096]{1,0:T(8,128)(2,1)}, u32[]{:S(2)}, u32[]{:S(2)}) %collective-permute-start.2) | collective-permute-done | bytes 4194336 | tf_op jit(solution)/shard_map/ppermute | solution.py:21
  1145.2 163.7 %all-gather.31.cloned.1.call-done = bf16[2048,4096]{1,0:T(8,128)(2,1)} async-done(((bf16[512,4096]{1,0:T(8,128)(2,1)}), bf16[2048,4096]{1,0:T(8,128)(2,1)}) %all-gather.31.cloned.1.call-update) | async-done | bytes 16777232 | tf_op jit(solution)/shard_map/all_gather | solution.py:142
  1332.5 262.9 %all-gather.29.cloned.1.call-done = bf16[2048,4096]{1,0:T(8,128)(2,1)} async-done(((bf16[512,4096]{1,0:T(8,128)(2,1)}), bf16[2048,4096]{1,0:T(8,128)(2,1)}) %all-gather.29.cloned.1.call-update) | async-done | bytes 16777232 | tf_op jit(solution)/shard_map/all_gather | solution.py:141
  1595.4 57.0 %all-gather.27.cloned.1.call-done = bf16[1024,2048]{1,0:T(8,128)(2,1)} async-done(((bf16[512,2048]{1,0:T(8,128)(2,1)}), bf16[1024,2048]{1,0:T(8,128)(2,1)}) %all-gather.27.cloned.1.call-update) | async-done | bytes 4194320 | tf_op jit(solution)/shard_map/all_gather | solution.py:86
  1676.7 36.2 multiply_convert_fusion.1
  1756.9 99.3 %reduce-scatter.20.cloned.1.call-done = f32[512,2048]{1,0:T(8,128)} async-done(((f32[1024,2048]{1,0:T(8,128)}), f32[512,2048]{1,0:T(8,128)}) %reduce-scatter.20.cloned.1.call-update) | async-done | bytes 4194320 | tf_op jit(solution)/shard_map/reduce_scatter | solution.py:90
  1865.0 56.6 %all-gather.35.cloned.1.call-done = bf16[1024,2048]{1,0:T(8,128)(2,1)} async-done(((bf16[512,2048]{1,0:T(8,128)(2,1)}), bf16[1024,2048]{1,0:T(8,128)(2,1)}) %all-gather.35.cloned.1.call-update) | async-done | bytes 4194320 | tf_op jit(solution)/shard_map/all_gather | solution.py:86
  1931.0 223.1 %while.52 = (s32[]{:T(128)}, f32[16,1024,1]{1,2,0:T(1,128)S(1)}, s32[4,1024]{1,0:T(4,128)S(1)}, s32[1024]{0:T(1024)S(1)}, s32[1024]{0:T(1024)S(1)}, /*index=5*/s...) while((s32[]{:T(128)}, f32[16,1024,1]{1,2,0:T(1,128)S(1)}, ...), condition=%wide.region_20.21_spmd.clone, body=%wide.region_18.20_spmd.clone.sunk | while | flops 4385163264 | bytes 145074336 | solution.py:247
  2154.1 522.8 %while.53 = (s32[]{:T(128)}, f32[1024,16,64]{0,2,1:T(8,128)}, bf16[4,1024,16,64]{1,3,2,0:T(8,128)(2,1)}, bf16[4,1024,16,64]{1,3,2,0:T(8,128)(2,1)}, bf16[4,1024,...) while((s32[]{:T(128)}, f32[1024,16,64]{0,2,1:T(8,128)}, ...), condition=%wide.region_22.23_spmd.clone, body=%wide.region_21.22_spmd.clone.sunk | while | flops 10915678208 | bytes 336832672 | solution.py:273
  2207.4 41.2 %fusion.197 = bf16[16,1024,1024]{1,2,0:T(8,128)(2,1)} fusion(f32[16,1024,1024]{2,1,0:T(8,128)} %fusion.196, f32[16,1024]{1,0:T(8,128)S(1)} %bitcast.308, f32[16,1024]{1,0:T(8,128)S(1)} %bitcast.307, pred[1024,1024]{0,1:T(8,128)(4,1)S(1)} %compare_and_fusion.11, bf16[1024,16,64]{0,2,1:T(8,128)(2,1)} %get-tuple-element.1279, ...), kind=kOutput, calls=%fused_computation.59.clone.2 | convolution fusion | flops 2248146944 | bytes 106037248 | tf_op jit(solution)/shard_map/while/body/eval_jaxpr/qhd,khd->hqk/dot_general | solution.py:252
  2337.0 41.2 %fusion.197 = bf16[16,1024,1024]{1,2,0:T(8,128)(2,1)} fusion(f32[16,1024,1024]{2,1,0:T(8,128)} %fusion.196, f32[16,1024]{1,0:T(8,128)S(1)} %bitcast.308, f32[16,1024]{1,0:T(8,128)S(1)} %bitcast.307, pred[1024,1024]{0,1:T(8,128)(4,1)S(1)} %compare_and_fusion.11, bf16[1024,16,64]{0,2,1:T(8,128)(2,1)} %get-tuple-element.1279, ...), kind=kOutput, calls=%fused_computation.59.clone.2 | convolution fusion | flops 2248146944 | bytes 106037248 | tf_op jit(solution)/shard_map/while/body/eval_jaxpr/qhd,khd->hqk/dot_general | solution.py:252
  2467.9 41.2 %fusion.197 = bf16[16,1024,1024]{1,2,0:T(8,128)(2,1)} fusion(f32[16,1024,1024]{2,1,0:T(8,128)} %fusion.196, f32[16,1024]{1,0:T(8,128)S(1)} %bitcast.308, f32[16,1024]{1,0:T(8,128)S(1)} %bitcast.307, pred[1024,1024]{0,1:T(8,128)(4,1)S(1)} %compare_and_fusion.11, bf16[1024,16,64]{0,2,1:T(8,128)(2,1)} %get-tuple-element.1279, ...), kind=kOutput, calls=%fused_computation.59.clone.2 | convolution fusion | flops 2248146944 | bytes 106037248 | tf_op jit(solution)/shard_map/while/body/eval_jaxpr/qhd,khd->hqk/dot_general | solution.py:252
  2598.7 41.2 %fusion.197 = bf16[16,1024,1024]{1,2,0:T(8,128)(2,1)} fusion(f32[16,1024,1024]{2,1,0:T(8,128)} %fusion.196, f32[16,1024]{1,0:T(8,128)S(1)} %bitcast.308, f32[16,1024]{1,0:T(8,128)S(1)} %bitcast.307, pred[1024,1024]{0,1:T(8,128)(4,1)S(1)} %compare_and_fusion.11, bf16[1024,16,64]{0,2,1:T(8,128)(2,1)} %get-tuple-element.1279, ...), kind=kOutput, calls=%fused_computation.59.clone.2 | convolution fusion | flops 2248146944 | bytes 106037248 | tf_op jit(solution)/shard_map/while/body/eval_jaxpr/qhd,khd->hqk/dot_general | solution.py:252
  2924.8 104.2 %reduce-scatter.40.cloned.1.call-done = bf16[128,4096]{1,0:T(8,128)(2,1)} async-done(((bf16[2048,4096]{1,0:T(8,128)(2,1)}), bf16[128,4096]{1,0:T(8,128)(2,1)}) %reduce-scatter.40.cloned.1.call-update) | async-done | bytes 1048592
  3032.2 178.3 %reduce-scatter.36.cloned.1.call-done = bf16[128,4096]{1,0:T(8,128)(2,1)} async-done(((bf16[2048,4096]{1,0:T(8,128)(2,1)}), bf16[128,4096]{1,0:T(8,128)(2,1)}) %reduce-scatter.36.cloned.1.call-update) | async-done | bytes 1048592 | tf_op jit(solution)/shard_map/reduce_scatter | solution.py:322
  3213.3 178.9 %reduce-scatter.38.cloned.1.call-done = bf16[128,4096]{1,0:T(8,128)(2,1)} async-done(((bf16[2048,4096]{1,0:T(8,128)(2,1)}), bf16[128,4096]{1,0:T(8,128)(2,1)}) %reduce-scatter.38.cloned.1.call-update) | async-done | bytes 1048592 | tf_op jit(solution)/shard_map/reduce_scatter | solution.py:325
  3395.0 72.6 %reduce-scatter.34.cloned.1.call-done = bf16[128,1024]{1,0:T(8,128)(2,1)} async-done(((bf16[2048,1024]{1,0:T(8,128)(2,1)}), bf16[128,1024]{1,0:T(8,128)(2,1)}) %reduce-scatter.34.cloned.1.call-update) | async-done | bytes 262160 | tf_op jit(solution)/shard_map/reduce_scatter | solution.py:319
  3469.4 74.4 %reduce-scatter.32.cloned.1.call-done = bf16[128,1024]{1,0:T(8,128)(2,1)} async-done(((bf16[2048,1024]{1,0:T(8,128)(2,1)}), bf16[128,1024]{1,0:T(8,128)(2,1)}) %reduce-scatter.32.cloned.1.call-update) | async-done | bytes 262160 | tf_op jit(solution)/shard_map/reduce_scatter | solution.py:316
  3545.5 73.6 %reduce-scatter.28.cloned.1.call-done = bf16[128,1024]{1,0:T(8,128)(2,1)} async-done(((bf16[2048,1024]{1,0:T(8,128)(2,1)}), bf16[128,1024]{1,0:T(8,128)(2,1)}) %reduce-scatter.28.cloned.1.call-update) | async-done | bytes 262160 | tf_op jit(solution)/shard_map/reduce_scatter | solution.py:310
  3621.0 74.4 %reduce-scatter.30.cloned.1.call-done = bf16[128,1024]{1,0:T(8,128)(2,1)} async-done(((bf16[2048,1024]{1,0:T(8,128)(2,1)}), bf16[128,1024]{1,0:T(8,128)(2,1)}) %reduce-scatter.30.cloned.1.call-update) | async-done | bytes 262160 | tf_op jit(solution)/shard_map/reduce_scatter | solution.py:313
  3697.1 98.6 %reduce-scatter.26.cloned.1.call-done = f32[512,2048]{1,0:T(8,128)} async-done(((f32[1024,2048]{1,0:T(8,128)}), f32[512,2048]{1,0:T(8,128)}) %reduce-scatter.26.cloned.1.call-update) | async-done | bytes 4194320 | tf_op jit(solution)/shard_map/reduce_scatter | solution.py:90
  3799.1 40.1 %all-reduce.2 = (f32[2048]{0:T(1024)S(1)}, f32[2048]{0:T(1024)S(1)}) all-reduce(f32[2048]{0:T(1024)S(1)} %get-tuple-element.665, f32[2048]{0:T(1024)S(1)} %copy-done.38), channel_id=8, replica_groups=mesh['fsdp'=4,'ctx'=4,'tensor'=2] {'fsdp','ctx','tensor'}, use_global_device_ids=true, to_apply=%region_28.29.clone | all-reduce | flops 4096 | bytes 32768
  3840.3 58.4 %reduce-scatter.18.cloned.1.call-done = f32[512,2048]{1,0:T(8,128)} async-done(((f32[1024,2048]{1,0:T(8,128)}), f32[512,2048]{1,0:T(8,128)}) %reduce-scatter.18.cloned.1.call-update) | async-done | bytes 4194320 | tf_op jit(solution)/shard_map/reduce_scatter | solution.py:90
  (371 shorter events, 1434.3 us)
Async XLA Ops:
  7.2 65.8 %all-gather.13.cloned.1.call-start = ((), (), s32[]{:S(2)}) async-start(), calls=%async_computation.13 | async-start | bytes 6291456 | tf_op jit(solution)/shard_map/all_gather | solution.py:86
  13.4 142.0 %all-gather.23.cloned.1.call-start = ((), (), s32[]{:S(2)}) async-start(), calls=%async_computation.18 | async-start | bytes 5242880 | tf_op jit(solution)/shard_map/all_gather | solution.py:134
  14.2 222.1 %all-gather.19.cloned.1.call-start = ((), (), s32[]{:S(2)}) async-start(), calls=%async_computation.16 | async-start | bytes 5242880 | tf_op jit(solution)/shard_map/all_gather | solution.py:135
  14.9 302.1 %all-gather.15.cloned.1.call-start = ((), (), s32[]{:S(2)}) async-start(), calls=%async_computation.14 | async-start | bytes 5242880 | tf_op jit(solution)/shard_map/all_gather | solution.py:136
  15.5 360.4 %all-gather.21.cloned.1.call-start = ((), (), s32[]{:S(2)}) async-start(), calls=%async_computation.17 | async-start | bytes 10485760 | tf_op jit(solution)/shard_map/all_gather | solution.py:154
  248.0 349.4 %all-gather.17.cloned.1.call-start = ((), (), s32[]{:S(2)}) async-start(), calls=%async_computation.15 | async-start | bytes 10485760 | tf_op jit(solution)/shard_map/all_gather | solution.py:155
  326.3 425.0 %all-gather.25.cloned.1.call-start = ((), (), s32[]{:S(2)}) async-start(), calls=%async_computation.19 | async-start | bytes 5242880 | tf_op jit(solution)/shard_map/all_gather | solution.py:137
  327.1 547.1 %reduce-scatter.16.cloned.1.call-start = ((), (), s32[]{:S(2)}) async-start(), calls=%async_computation.20 | async-start | bytes 12582912 | tf_op jit(solution)/shard_map/reduce_scatter | solution.py:90
  762.0 383.1 %all-gather.33.cloned.1.call-start = ((), (), s32[]{:S(2)}) async-start(), calls=%async_computation.25 | async-start | bytes 6291456 | tf_op jit(solution)/shard_map/all_gather | solution.py:86
  762.8 546.1 %all-gather.31.cloned.1.call-start = ((), (), s32[]{:S(2)}) async-start(), calls=%async_computation.23 | async-start | bytes 20971520 | tf_op jit(solution)/shard_map/all_gather | solution.py:142
  763.4 832.0 %all-gather.29.cloned.1.call-start = ((), (), s32[]{:S(2)}) async-start(), calls=%async_computation.22 | async-start | bytes 20971520 | tf_op jit(solution)/shard_map/all_gather | solution.py:141
  764.1 888.3 %all-gather.27.cloned.1.call-start = ((), (), s32[]{:S(2)}) async-start(), calls=%async_computation.21 | async-start | bytes 6291456 | tf_op jit(solution)/shard_map/all_gather | solution.py:86
  764.1 95.6 %collective-permute-start = (bf16[512,4096]{1,0:T(8,128)(2,1)}, bf16[512,4096]{1,0:T(8,128)(2,1)}, u32[]{:S(2)}, u32[]{:S(2)}) collective-permute-start(bf16[512,4096]{1,0:T(8,128)(2,1)} %param.28), channel_id=1, source_target_pairs={{0,8},{8,16},{16,24},{24,0},{1,9},{9,17},{17,25},{25,1},{2,10},{10... | collective-permute-start | bytes 12582920 | tf_op jit(solution)/shard_map/ppermute | solution.py:21
  765.7 219.3 %collective-permute-start.1 = (bf16[512,4096]{1,0:T(8,128)(2,1)}, bf16[512,4096]{1,0:T(8,128)(2,1)}, u32[]{:S(2)}, u32[]{:S(2)}) collective-permute-start(bf16[512,4096]{1,0:T(8,128)(2,1)} %param.28), channel_id=1, source_target_pairs={{0,24},{8,0},{16,8},{24,16},{1,25},{9,1},{17,9},{25,17},{2,26},{10... | collective-permute-start | bytes 12582920 | tf_op jit(solution)/shard_map/ppermute | solution.py:24
  859.8 280.7 %collective-permute-start.2 = (bf16[512,4096]{1,0:T(8,128)(2,1)}, bf16[512,4096]{1,0:T(8,128)(2,1)}, u32[]{:S(2)}, u32[]{:S(2)}) collective-permute-start(bf16[512,4096]{1,0:T(8,128)(2,1)} %collective-permute-done), channel_id=1, source_target_pairs={{0,8},{8,16},{16,24},{24,0},{1,9},{9,17},{17,25},{25,1},{2,10},{10... | collective-permute-start | bytes 12582920 | tf_op jit(solution)/shard_map/ppermute | solution.py:21
  881.1 975.2 %reduce-scatter.20.cloned.1.call-start = ((), (), s32[]{:S(2)}) async-start(), calls=%async_computation.26 | async-start | bytes 12582912 | tf_op jit(solution)/shard_map/reduce_scatter | solution.py:90
  1756.9 164.7 %all-gather.35.cloned.1.call-start = ((), (), s32[]{:S(2)}) async-start(), calls=%async_computation.27 | async-start | bytes 6291456 | tf_op jit(solution)/shard_map/all_gather | solution.py:86
  1864.7 967.3 %reduce-scatter.24.cloned.1.call-start = ((), (), s32[]{:S(2)}) async-start(), calls=%async_computation.29 | async-start | bytes 10485760 | tf_op jit(solution)/shard_map/reduce_scatter | solution.py:283
  2700.2 146.3 %reduce-scatter.22.cloned.1.call-start = ((), (), s32[]{:S(2)}) async-start(), calls=%async_computation.28 | async-start | bytes 10485760 | tf_op jit(solution)/shard_map/reduce_scatter | solution.py:277
  2725.2 303.8 %reduce-scatter.40.cloned.1.call-start = ((), (), s32[]{:S(2)}) async-start(), calls=%async_computation.37 | async-start | bytes 17825792
  2770.8 439.7 %reduce-scatter.36.cloned.1.call-start = ((), (), s32[]{:S(2)}) async-start(), calls=%async_computation.35 | async-start | bytes 17825792 | tf_op jit(solution)/shard_map/reduce_scatter | solution.py:322
  2795.9 596.3 %reduce-scatter.38.cloned.1.call-start = ((), (), s32[]{:S(2)}) async-start(), calls=%async_computation.36 | async-start | bytes 17825792 | tf_op jit(solution)/shard_map/reduce_scatter | solution.py:325
  2821.5 646.1 %reduce-scatter.34.cloned.1.call-start = ((), (), s32[]{:S(2)}) async-start(), calls=%async_computation.34 | async-start | bytes 4456448 | tf_op jit(solution)/shard_map/reduce_scatter | solution.py:319
  2831.7 712.0 %reduce-scatter.32.cloned.1.call-start = ((), (), s32[]{:S(2)}) async-start(), calls=%async_computation.33 | async-start | bytes 4456448 | tf_op jit(solution)/shard_map/reduce_scatter | solution.py:316
  2841.5 777.7 %reduce-scatter.28.cloned.1.call-start = ((), (), s32[]{:S(2)}) async-start(), calls=%async_computation.31 | async-start | bytes 4456448 | tf_op jit(solution)/shard_map/reduce_scatter | solution.py:310
  2860.1 835.3 %reduce-scatter.30.cloned.1.call-start = ((), (), s32[]{:S(2)}) async-start(), calls=%async_computation.32 | async-start | bytes 4456448 | tf_op jit(solution)/shard_map/reduce_scatter | solution.py:313
  2870.3 925.5 %reduce-scatter.26.cloned.1.call-start = ((), (), s32[]{:S(2)}) async-start(), calls=%async_computation.30 | async-start | bytes 12582912 | tf_op jit(solution)/shard_map/reduce_scatter | solution.py:90
  2900.3 998.3 %reduce-scatter.18.cloned.1.call-start = ((), (), s32[]{:S(2)}) async-start(), calls=%async_computation.24 | async-start | bytes 12582912 | tf_op jit(solution)/shard_map/reduce_scatter | solution.py:90
  3032.2 763.6 %copy-start.6 = (bf16[512,2048]{1,0:T(8,128)(2,1)S(1)}, bf16[512,2048]{1,0:T(8,128)(2,1)}, u32[]{:S(2)}) copy-start(bf16[512,2048]{1,0:T(8,128)(2,1)} %param.21) | copy-start | bytes 6291460
  3032.2 763.6 %copy-start.30 = (f32[2048]{0:T(1024)S(1)}, f32[2048]{0:T(1024)}, u32[]{:S(2)}) copy-start(f32[2048]{0:T(1024)} %param.22) | copy-start | bytes 24580
  3032.2 763.6 %copy-start.37 = (f32[512]{0:T(512)S(1)}, f32[512]{0:T(512)}, u32[]{:S(2)}) copy-start(f32[512]{0:T(512)} %copy-done.36) | copy-start | bytes 6148
  3469.3 429.3 %copy-start.40 = (f32[512]{0:T(512)S(1)}, f32[512]{0:T(512)}, u32[]{:S(2)}) copy-start(f32[512]{0:T(512)} %copy-done.39) | copy-start | bytes 6148
  (47 other events, 2693.4 us)
Sparse Core Ops, SparseCore 0:
  13.5 59.4 all-gather.12
  74.6 80.7 all-gather.22
  156.9 79.2 all-gather.18
  237.7 79.2 all-gather.14
  319.0 56.8 all-gather.20
  377.9 58.2 all-gather.16
  437.7 80.7 all-gather.24
  762.1 99.2 reduce-scatter.15
  863.1 56.7 all-gather.32
  921.3 387.5 all-gather.30
  1310.5 284.7 all-gather.28
  1597.4 54.9 all-gather.26
  1757.0 99.2 reduce-scatter.19
  1864.8 56.7 all-gather.34
  2700.3 71.7 reduce-scatter.23
  2774.7 71.7 reduce-scatter.21
  2850.4 178.5 reduce-scatter.39
  3032.9 177.5 reduce-scatter.35
  3214.6 177.5 reduce-scatter.37
  3395.9 71.5 reduce-scatter.33
  3471.9 71.7 reduce-scatter.31
  3547.6 71.5 reduce-scatter.27
  3623.5 71.7 reduce-scatter.29
  3697.5 98.2 reduce-scatter.25
  3798.2 100.4 reduce-scatter.17
